TPU v7x, 512 devices: a whole 4x4x16 slice. The times are simulated.
512 devices in a mesh: node: 64 (over y, z), local: 8 (over x, core).
Axes of the slice: x: 4, y: 4, z: 16, core: 2. Of those that a mesh axis runs over, the one named last changes fastest.
Arguments:
- grad_out: bfloat16 [65536, 3584], P(('node', 'local')), may hold values from -6 to 6
- expert_ids: int32 [65536, 8], P(('node', 'local')), may hold values from 0 to 255, as said below
- gate_weights: float32 [65536, 8], P(('node', 'local')), may hold values from 0.05 to 0.35
- saved_hidden: bfloat16 [64, 1024, 1024], P('node', None, 'local'), may hold values from -0.59765625 to 0.59765625
- down_weight: bfloat16 [64, 1024, 3584], P('node', 'local'), may hold values from -0.1875 to 0.1875
- second_moment: bfloat16 [64, 1024, 3584], P('node', 'local'), may hold values from 0.0019989014 to 0.25
Outputs:
- gate_weight_gradient: float32 [65536, 8], P(('node', 'local'))
- hidden_grad: bfloat16 [64, 1024, 1024], P('node', None, 'local')
- new_weight: bfloat16 [64, 1024, 3584], P('node', 'local')
- new_second: bfloat16 [64, 1024, 3584], P('node', 'local')
Inputs may be any that keep to these rules, and one draw needn't show every extreme that they name: `expert_ids`: each row names 8 different experts on at most 4 nodes (node = id // 4), two on each; at most one per row is in flight (id % 4 == 0). Among the rows of one device at most 2 name the in-flight expert of any one node, and in every draw some node receives exactly 2 from every device.
All inputs are finite; a program needn't handle non-finite values.
Results may differ from a plain program's by a relative error of at most 0.0051.
Values may be sent and summed in bfloat16 or wider, within the bound.
No kernel may reach another device: no remote copies, remote signals or barrier semaphores. Data moves between devices by JAX's collectives and lax.ppermute only.
A program may use at most 128 MiB of HBM per device.

v0:
```python
import jax
import jax.numpy as jnp
from jax import lax
from jax.sharding import PartitionSpec as P

EXPERTS_PER_HOST = 4
CAP = 2
beta_second = 0.95
learn_rate = 0.002
decay_rate = 0.1
epsilon = 1e-08
correct_second = 0.994079470779666


def gather_rows(picked_experts, gate_values, grads, node_count):
    transit_rows = picked_experts % EXPERTS_PER_HOST == 0
    row_present = jnp.any(transit_rows, 1)
    destination_node = jnp.sum(jnp.where(transit_rows, picked_experts // EXPERTS_PER_HOST, 0), 1)
    onehot = (
        (destination_node[:, None] == jnp.arange(node_count, dtype=jnp.int32)[None, :])
        & row_present[:, None]
    ).astype(jnp.int32)
    within_rank = jnp.sum(onehot * (jnp.cumsum(onehot, 0) - 1), 1)
    slot_index = destination_node * CAP + within_rank
    expert_location = (
        jnp.arange(node_count * CAP, dtype=jnp.int32)[:, None] == slot_index[None, :]
    ) & row_present[None, :]
    matched_gate = jnp.sum(jnp.where(transit_rows, gate_values, 0.0), 1).astype(jnp.bfloat16)
    departing_rows = jnp.dot(
        expert_location.astype(jnp.bfloat16), grads, preferred_element_type=jnp.float32
    ).astype(jnp.bfloat16)
    departing_gates = jnp.sum(
        jnp.where(expert_location, matched_gate.astype(jnp.float32)[None, :], 0.0), 1
    ).astype(jnp.bfloat16)
    feature_count = grads.shape[1]
    return (
        departing_rows.reshape(node_count, CAP, feature_count),
        departing_gates.reshape(node_count, CAP),
        expert_location,
        transit_rows,
    )


def on_device(grad_out, expert_ids, gate_weights, saved_hidden, down_weight, second_moment):
    node_count = lax.axis_size("node")
    members = lax.axis_size("local")
    feature_count = grad_out.shape[1]
    departing_rows, departing_gates, expert_location, transit_rows = gather_rows(
        expert_ids, gate_weights, grad_out, node_count
    )
    copies, copy_gates = (
        lax.all_gather(departing_rows[None], "local", axis=0, tiled=True),
        lax.all_gather(departing_gates[None], "local", axis=0, tiled=True),
    )
    arrived, arrived_gates = (
        lax.all_to_all(copies, "node", split_axis=1, concat_axis=1, tiled=True),
        lax.all_to_all(copy_gates, "node", split_axis=1, concat_axis=1, tiled=True),
    )
    arrived_rows = arrived.reshape(-1, feature_count)
    slot_gates = arrived_gates.reshape(-1).astype(jnp.float32)
    weight_now = down_weight[0]
    hidden_now = saved_hidden[0]
    unscaled = lax.dot_general(
        arrived_rows, weight_now, (((1,), (1,)), ((), ())), preferred_element_type=jnp.float32
    )
    hidden_out = (slot_gates[:, None] * unscaled).astype(jnp.bfloat16)
    slot_score = jnp.sum(unscaled * hidden_now.astype(jnp.float32), 1)
    scaled = (slot_gates[:, None] * arrived_rows.astype(jnp.float32)).astype(jnp.bfloat16)
    grad = lax.dot_general(
        hidden_now, scaled, (((0,), (0,)), ((), ())), preferred_element_type=jnp.float32
    )
    second_new = (
        beta_second * second_moment[0].astype(jnp.float32) + (1.0 - beta_second) * grad * grad
    )
    weight_f = weight_now.astype(jnp.float32)
    update = grad / (jnp.sqrt(second_new / correct_second) + epsilon) + decay_rate * weight_f
    weight_new = weight_f - learn_rate * update
    score_terms = slot_score.reshape(members, node_count * CAP)
    summed = lax.psum(score_terms, "local")
    own_terms = lax.dynamic_slice_in_dim(summed, lax.axis_index("local"), 1, 0)
    returned = lax.all_to_all(
        own_terms.reshape(node_count, CAP), "node", split_axis=0, concat_axis=0, tiled=True
    )
    returned_flat = returned.reshape(node_count * CAP)
    token_gradient = jnp.sum(jnp.where(expert_location, returned_flat[:, None], 0.0), 0)
    gate_weight_gradient = jnp.where(transit_rows, token_gradient[:, None], 0.0)
    return (
        gate_weight_gradient,
        hidden_out[None],
        weight_new.astype(jnp.bfloat16)[None],
        second_new.astype(jnp.bfloat16)[None],
    )


def solution(mesh):
    return jax.shard_map(
        on_device,
        mesh=mesh,
        in_specs=(
            P(("node", "local"), None),
            P(("node", "local"), None),
            P(("node", "local"), None),
            P("node", None, "local"),
            P("node", "local", None),
            P("node", "local", None),
        ),
        out_specs=(
            P(("node", "local"), None),
            P("node", None, "local"),
            P("node", "local", None),
            P("node", "local", None),
        ),
        check_vma=False,
    )
```

profile of v0, /device:TPU:2, one launch (start us, length us, event | category | flops | bytes accessed | tf_op | source)
XLA Modules:
  0.0 566.0 jit_solution(3273625820910826075)
XLA Ops:
  7.2 0.0 copy-start
  7.2 0.0 all-gather.2.cloned.1.call-start
  7.2 0.8 fusion.22
  8.0 0.7 fusion.19
  8.7 0.1 fusion.14
  8.8 0.2 reduce_window_sum.11
  9.0 0.2 select_reduce_fusion.2
  9.2 0.4 convolution_convert_fusion
  9.6 0.3 broadcast_in_dim_reshape.2
  9.9 1.0 copy.65
  11.0 0.0 all-gather.2.cloned.1.call-update
  11.0 56.7 %all-gather.2.cloned.1.call-done = bf16[8,64,2,3584]{3,1,2,0:T(8,128)(2,1)} async-done(((bf16[1,64,2,3584]{3,1,2,0:T(8,128)(2,1)}), bf16[8,64,2,3584]{3,1,2,0:T(8,128)(2,1)}) %all-gather.2.cloned.1.call-update) | async-done | bytes 7340048 | tf_op jit(solution)/shard_map/all_gather | solution.py:52
  67.7 14.7 %copy.66 = bf16[8,64,2,3584]{3,2,0,1:T(2,128)(2,1)} copy(bf16[8,64,2,3584]{3,1,2,0:T(8,128)(2,1)} %all-gather.2.cloned.1.call-done) | data formatting | bytes 14680064 | tf_op jit(solution)/shard_map/all_gather | solution.py:52
  82.4 16.0 %all-to-all-start = ((bf16[8,64,2,3584]{3,2,0,1:T(2,128)(2,1)}), bf16[8,64,2,3584]{3,2,0,1:T(2,128)(2,1)}, u32[]{:S(2)}, u32[]{:S(2)}) async-start(bf16[8,64,2,3584]{3,2,0,1:T(2,128)(2,1)} %copy.66), calls=%async_computation | async-start | bytes 14680064 | tf_op jit(solution)/shard_map/all_to_all | solution.py:56
  98.4 0.1 copy.69
  98.6 323.8 %all-to-all-done = bf16[8,64,2,3584]{3,2,0,1:T(2,128)(2,1)} async-done(((bf16[8,64,2,3584]{3,2,0,1:T(2,128)(2,1)}), bf16[8,64,2,3584]{3,2,0,1:T(2,128)(2,1)}, u32[]{:S(2)}, u32[]{:S(2)}) %all-to-all-start) | async-done | bytes 7340064 | tf_op jit(solution)/shard_map/all_to_all | solution.py:56
  422.4 7.4 %copy.67 = bf16[8,64,2,3584]{3,2,1,0:T(2,128)(2,1)} copy(bf16[8,64,2,3584]{3,2,0,1:T(2,128)(2,1)} %all-to-all-done) | data formatting | bytes 14680064 | tf_op jit(solution)/shard_map/all_to_all | solution.py:56
  429.8 15.5 %reshape.62 = bf16[1024,3584]{1,0:T(8,128)(2,1)} reshape(bf16[8,64,2,3584]{3,2,1,0:T(2,128)(2,1)} %copy.67) | data formatting | bytes 14680064 | tf_op jit(solution)/shard_map/reshape | solution.py:59
  445.4 5.6 multiply_reduce_fusion
  451.0 10.5 %psum.7 = f32[8,128]{1,0:T(8,128)S(1)} all-reduce(f32[8,128]{1,0:T(8,128)S(1)} %bitcast.41), channel_id=1, replica_groups=mesh['node'=64,'local'=8] {'local'}, use_global_device_ids=true, to_apply=%region_5.6 | all-reduce | flops 1024 | bytes 8192 | tf_op jit(solution)/shard_map/psum | solution.py:79
  461.5 0.8 all_to_all.13
  462.2 7.0 %all-to-all-start.1 = ((f32[64,1,2]{2,1,0:T(1,128)}), f32[64,1,2]{2,1,0:T(1,128)}, u32[]{:S(2)}, u32[]{:S(2)}) async-start(f32[64,1,2]{2,1,0:T(1,128)} %bitcast.3), calls=%async_computation.1 | async-start | bytes 65536 | tf_op jit(solution)/shard_map/all_to_all | solution.py:81
  469.2 0.5 select_reduce_fusion.3
  469.8 0.6 copy.68
  470.4 0.7 convert_element_type.132
  471.1 0.6 copy.78
  471.7 11.6 %all-to-all-done.1 = f32[64,1,2]{2,1,0:T(1,128)} async-done(((f32[64,1,2]{2,1,0:T(1,128)}), f32[64,1,2]{2,1,0:T(1,128)}, u32[]{:S(2)}, u32[]{:S(2)}) %all-to-all-start.1) | async-done | bytes 544 | tf_op jit(solution)/shard_map/all_to_all | solution.py:81
  483.3 0.5 broadcast.47
  483.8 1.5 reduce.7
  485.3 0.1 broadcast_in_dim.59
  485.4 0.1 select_reduce_fusion
  485.6 0.2 convert_element_type.82
  485.7 0.1 copy.71
  485.8 11.1 %all_gather.7 = bf16[8,64,2]{1,2,0:T(2,128)(2,1)S(1)} all-gather(bf16[1,64,2]{1,2,0:T(2,128)(2,1)S(1)} %copy.71), channel_id=1, replica_groups=mesh['node'=64,'local'=8] {'local'}, dimensions={0}, use_global_device_ids=true | all-gather | bytes 2304 | tf_op jit(solution)/shard_map/all_gather | solution.py:53
  496.9 0.7 copy.72
  497.6 4.8 all-to-all-start.2
  502.4 0.6 broadcast_select_fusion
  503.0 13.6 %all-to-all-done.2 = bf16[8,64,2]{0,2,1:T(2,128)(2,1)S(1)} async-done(((bf16[8,64,2]{0,2,1:T(2,128)(2,1)}), bf16[8,64,2]{0,2,1:T(2,128)(2,1)S(1)}, u32[]{:S(2)}, u32[]{:S(2)}) %all-to-all-start.2) | async-done | bytes 2080 | tf_op jit(solution)/shard_map/all_to_all | solution.py:57
  516.6 0.1 copy.73
  516.7 0.2 copy.74
  516.8 7.8 %multiply_convert_fusion = bf16[8,64,2,3584]{3,1,2,0:T(8,128)(2,1)S(1)} fusion(bf16[8,64,2,3584]{3,2,0,1:T(2,128)(2,1)} %all-to-all-done, f32[8,64,2]{1,2,0:T(2,128)S(1)} %copy.75), kind=kLoop, calls=%fused_computation | loop fusion | flops 11010048 | bytes 14684160 | tf_op jit(solution)/shard_map/convert_element_type | solution.py:68
  524.6 7.1 %copy.77 = bf16[8,64,2,3584]{3,2,1,0:T(2,128)(2,1)} copy(bf16[8,64,2,3584]{3,1,2,0:T(8,128)(2,1)S(1)} %multiply_convert_fusion) | data formatting | bytes 14680064 | tf_op jit(solution)/shard_map/convert_element_type | solution.py:68
  531.7 15.4 %convert_element_type.90 = bf16[1024,3584]{1,0:T(8,128)(2,1)} reshape(bf16[8,64,2,3584]{3,2,1,0:T(2,128)(2,1)} %copy.77) | data formatting | bytes 14680064 | tf_op jit(solution)/shard_map/convert_element_type | solution.py:68
  547.1 7.3 %fusion.5 = (bf16[1,128,3584]{1,2,0:T(8,128)(2,1)}, bf16[1,128,3584]{1,2,0:T(8,128)(2,1)}) fusion(bf16[1,128,3584]{1,2,0:T(8,128)(2,1)S(1)} %copy.78, bf16[1,128,3584]{1,2,0:T(8,128)(2,1)S(1)} %copy.68, bf16[1024,3584]{1,0:T(8,128)(2,1)} %convert_element_type.90, bf16[1,1024,128]{2,1,0:T(8,128)(2,1)S(1)} %copy-done.5), kind=kOutput, calls=%fused_computation.11 | convolution fusion | flops 946405376 | bytes 11272192 | tf_op jit(solution)/shard_map/dot_general | solution.py:69
  554.5 2.3 copy.80
  556.8 1.3 copy.81
  558.1 0.2 reshape.64
  558.3 0.8 copy.79
  (17 shorter events, 0.1 us)
Async XLA Ops:
  7.2 2.0 copy-start
  7.2 60.5 %all-gather.2.cloned.1.call-start = ((), (), s32[]{:S(2)}) async-start(), calls=%async_computation.3 | async-start | bytes 8257536 | tf_op jit(solution)/shard_map/all_gather | solution.py:52
  82.4 16.0 %copy-start.5 = (bf16[1,1024,128]{2,1,0:T(8,128)(2,1)S(1)}, bf16[1,1024,128]{2,1,0:T(8,128)(2,1)}, u32[]{:S(2)}) copy-start(bf16[1,1024,128]{2,1,0:T(8,128)(2,1)} %param.9) | copy-start | bytes 786436
  82.4 340.0 %all-to-all-start = ((bf16[8,64,2,3584]{3,2,0,1:T(2,128)(2,1)}), bf16[8,64,2,3584]{3,2,0,1:T(2,128)(2,1)}, u32[]{:S(2)}, u32[]{:S(2)}) async-start(bf16[8,64,2,3584]{3,2,0,1:T(2,128)(2,1)} %copy.66), calls=%async_computation | async-start | bytes 14680064 | tf_op jit(solution)/shard_map/all_to_all | solution.py:56
  429.8 15.5 %copy-start.2 = (bf16[1,128,3584]{2,1,0:T(8,128)(2,1)S(1)}, bf16[1,128,3584]{2,1,0:T(8,128)(2,1)}, u32[]{:S(2)}) copy-start(bf16[1,128,3584]{2,1,0:T(8,128)(2,1)} %param.10) | copy-start | bytes 2752516
  445.4 23.9 %copy-start.6 = (f32[128,8]{0,1:T(8,128)S(1)}, f32[128,8]{0,1:T(8,128)}, u32[]{:S(2)}) copy-start(f32[128,8]{0,1:T(8,128)} %param.8) | copy-start | bytes 12292
  450.9 20.1 %copy-start.3 = (bf16[1,128,3584]{2,1,0:T(8,128)(2,1)S(1)}, bf16[1,128,3584]{2,1,0:T(8,128)(2,1)}, u32[]{:S(2)}) copy-start(bf16[1,128,3584]{2,1,0:T(8,128)(2,1)} %param.11) | copy-start | bytes 2752516
  462.2 21.0 %all-to-all-start.1 = ((f32[64,1,2]{2,1,0:T(1,128)}), f32[64,1,2]{2,1,0:T(1,128)}, u32[]{:S(2)}, u32[]{:S(2)}) async-start(f32[64,1,2]{2,1,0:T(1,128)} %bitcast.3), calls=%async_computation.1 | async-start | bytes 65536 | tf_op jit(solution)/shard_map/all_to_all | solution.py:81
  497.6 19.0 %all-to-all-start.2 = ((bf16[8,64,2]{0,2,1:T(2,128)(2,1)}), bf16[8,64,2]{0,2,1:T(2,128)(2,1)S(1)}, u32[]{:S(2)}, u32[]{:S(2)}) async-start(bf16[8,64,2]{0,2,1:T(2,128)(2,1)} %copy.72), calls=%async_computation.2 | async-start | bytes 65536 | tf_op jit(solution)/shard_map/all_to_all | solution.py:57
  554.5 2.4 copy-start.4
  554.5 4.7 copy-start.1
Sparse Core Ops, SparseCore 0:
  11.1 56.5 all-gather.1
where the time goes:
time: 567 us; the launch traced here: 566 us
  waiting for transfers between devices  406 us (72%)
  local copies, waits for them, and re-layouts  70.1 us (12%)
  starting transfers between devices  27.8 us (5%)
  blocking collectives  21.6 us (4%)
  between operations  14.2 us (3%)
  matrix products  13.3 us (2%)
  other arithmetic  13.2 us (2%)
    all_to_all x1, waiting for transfers between devices, on_device(): lax.all_to_all(copies, 'node', split_axis=1, concat_axis=1, tiled=True)  324 us
    all_gather x1, waiting for transfers between devices, on_device(): lax.all_gather(departing_rows[None], 'local', axis=0, tiled=True)  56.7 us
    convert_element_type x2, local copies, waits for them, and re-layouts, on_device(): (slot_gates[:, None] * arrived_rows.astype(jnp.float32)).astype(jnp.bfloa...  22.5 us
    all_to_all x1, starting transfers between devices, on_device(): lax.all_to_all(copies, 'node', split_axis=1, concat_axis=1, tiled=True)  16 us
    reshape x1, local copies, waits for them, and re-layouts, on_device(): arrived_rows = arrived.reshape(-1, feature_count)  15.5 us
    all_gather x1, local copies, waits for them, and re-layouts, on_device(): lax.all_gather(departing_rows[None], 'local', axis=0, tiled=True)  14.7 us
    all_to_all x1, waiting for transfers between devices, on_device(): lax.all_to_all(copy_gates, 'node', split_axis=1, concat_axis=1, tiled=True)  13.6 us
    all_to_all x1, waiting for transfers between devices, on_device(): lax.all_to_all(own_terms.reshape(node_count, CAP), 'node', split_axis=0,...  11.6 us
  transfers between devices with their start and end apart: 4, of which 4 were waited for; matrix products, arithmetic and copies ran while one was open for 1% of the time, Pallas kernels for 0%

commit v1 on v0

--- a/solution.py
+++ b/solution.py
@@ -10,6 +10,24 @@
 decay_rate = 0.1
 epsilon = 1e-08
 correct_second = 0.994079470779666
+
+
+def collect(array, axis, dim):
+    ways, here, hop = (lax.axis_size(axis), lax.axis_index(axis), array.shape[dim])
+    dims = [n * ways if d == dim else n for d, n in enumerate(array.shape)]
+    full = lax.dynamic_update_slice_in_dim(
+        jnp.zeros(dims, array.dtype), array, here * hop, axis=dim
+    )
+    going_up = going_down = array
+    for far in range(1, ways // 2 + 1):
+        going_up = lax.ppermute(going_up, axis, [(d, (d + 1) % ways) for d in range(ways)])
+        full = lax.dynamic_update_slice_in_dim(full, going_up, (here - far) % ways * hop, axis=dim)
+        if 2 * far < ways:
+            going_down = lax.ppermute(going_down, axis, [(d, (d - 1) % ways) for d in range(ways)])
+            full = lax.dynamic_update_slice_in_dim(
+                full, going_down, (here + far) % ways * hop, axis=dim
+            )
+    return full
 
 
 def gather_rows(picked_experts, gate_values, grads, node_count):
@@ -49,7 +67,7 @@
         expert_ids, gate_weights, grad_out, node_count
     )
     copies, copy_gates = (
-        lax.all_gather(departing_rows[None], "local", axis=0, tiled=True),
+        collect(departing_rows[None], "local", 0),
         lax.all_gather(departing_gates[None], "local", axis=0, tiled=True),
     )
     arrived, arrived_gates = (

time: 567 us -> 541 us (0.954)
  waiting for transfers between devices: 406 us -> 375 us
  between operations: 14.2 us -> 0.82 us
  starting transfers between devices: 27.8 us -> 38.8 us
  local copies, waits for them, and re-layouts: 70.1 us -> 76.5 us
    all_gather x1 -> x0, waiting for transfers between devices: 56.7 us -> none  [on_device(): lax.all_gather(departing_rows[None], 'local', axis=0, tiled=True)]
    ppermute x0 -> x7, waiting for transfers between devices: none -> 26.7 us  [the longest x4 26.7 us: collect(): lax.ppermute(going_up, axis, [(d, (d + 1) % ways) for d in range(ways)])]
    all_gather x1 -> x0, local copies, waits for them, and re-layouts: 14.7 us -> none  [on_device(): lax.all_gather(departing_rows[None], 'local', axis=0, tiled=True)]
    dynamic_update_slice x0 -> x8, local copies, waits for them, and re-layouts: none -> 13 us  [the longest x4 6.49 us: collect(): lax.dynamic_update_slice_in_dim(full, going_up, (here - far) % ways * hop...]
    broadcast_in_dim x0 -> x1, local copies, waits for them, and re-layouts: none -> 7.57 us  [collect(): jnp.zeros(dims, array.dtype)]
    ppermute x0 -> x7, starting transfers between devices: none -> 6.24 us  [the longest x3 6.21 us: collect(): lax.ppermute(going_down, axis, [(d, (d - 1) % ways) for d in range(ways)])]
  transfers between devices with their start and end apart: 4 -> 10, of which waited for: 4 -> 7; matrix products, arithmetic and copies ran while one was open for 1% -> 4% of each run, Pallas kernels for 0% -> 0%
where the time goes in v1:
time: 541 us; the launch traced here: 540 us
  waiting for transfers between devices  375 us (69%)
  local copies, waits for them, and re-layouts  76.5 us (14%)
  starting transfers between devices  38.8 us (7%)
  blocking collectives  23.8 us (4%)
  matrix products  13.6 us (3%)
  other arithmetic  12 us (2%)
    all_to_all x1, waiting for transfers between devices, on_device(): lax.all_to_all(copies, 'node', split_axis=1, concat_axis=1, tiled=True)  322 us
    ppermute x4, waiting for transfers between devices, collect(): lax.ppermute(going_up, axis, [(d, (d + 1) % ways) for d in range(ways)])  26.7 us
    convert_element_type x2, local copies, waits for them, and re-layouts, on_device(): (slot_gates[:, None] * arrived_rows.astype(jnp.float32)).astype(jnp.bfloa...  22.5 us
    all_to_all x1, starting transfers between devices, on_device(): lax.all_to_all(copies, 'node', split_axis=1, concat_axis=1, tiled=True)  18.4 us
    reshape x1, local copies, waits for them, and re-layouts, on_device(): arrived_rows = arrived.reshape(-1, feature_count)  15.5 us
    all_to_all x1, waiting for transfers between devices, on_device(): lax.all_to_all(copy_gates, 'node', split_axis=1, concat_axis=1, tiled=True)  13.8 us
    psum x1, blocking collectives, on_device(): summed = lax.psum(score_terms, 'local')  12.6 us
    all_to_all x1, waiting for transfers between devices, on_device(): lax.all_to_all(own_terms.reshape(node_count, CAP), 'node', split_axis=0,...  12.1 us
  transfers between devices with their start and end apart: 10, of which 7 were waited for; matrix products, arithmetic and copies ran while one was open for 4% of the time, Pallas kernels for 0%

profile of v1, /device:TPU:2, one launch (start us, length us, event | category | flops | bytes accessed | tf_op | source)
XLA Modules:
  0.0 540.1 jit_solution(12609895979391699327)
XLA Ops:
  0.6 0.8 fusion.23
  1.4 0.7 fusion.19
  2.3 0.2 reduce_window_sum.11
  2.4 0.2 select_reduce_fusion.2
  2.6 0.4 convolution_convert_fusion
  3.0 0.3 broadcast_in_dim_reshape.2
  3.4 1.7 collective-permute-start.1
  5.1 7.6 %broadcast_in_dim.62 = bf16[8,64,2,3584]{3,2,0,1:T(2,128)(2,1)} broadcast(bf16[]{:T(256)} %constant.92.clone.1), dimensions={} | broadcast | bytes 7340034 | tf_op jit(solution)/shard_map/broadcast_in_dim | solution.py:19
  12.7 1.6 constant_dynamic-update-slice_fusion.7
  14.3 1.9 collective-permute-done
  16.2 2.4 collective-permute-start.3
  18.6 1.6 constant_dynamic-update-slice_fusion.6
  20.3 1.7 constant_dynamic-update-slice_fusion.5
  21.9 7.8 %collective-permute-done.2 = bf16[1,64,2,3584]{3,2,0,1:T(2,128)(2,1)S(1)} collective-permute-done((bf16[1,64,2,3584]{3,2,0,1:T(2,128)(2,1)S(1)}, bf16[1,64,2,3584]{3,2,0,1:T(2,128)(2,1)S(1)}, u32[]{:S(2)}, u32[]{:S(2)}) %collective-permute-start.2) | collective-permute-done | bytes 917536 | tf_op jit(solution)/shard_map/ppermute | solution.py:23
  29.7 2.0 collective-permute-start.5
  31.8 1.6 constant_dynamic-update-slice_fusion.4
  33.4 1.6 constant_dynamic-update-slice_fusion.3
  35.0 7.5 %collective-permute-done.4 = bf16[1,64,2,3584]{3,2,0,1:T(2,128)(2,1)S(1)} collective-permute-done((bf16[1,64,2,3584]{3,2,0,1:T(2,128)(2,1)S(1)}, bf16[1,64,2,3584]{3,2,0,1:T(2,128)(2,1)S(1)}, u32[]{:S(2)}, u32[]{:S(2)}) %collective-permute-start.4) | collective-permute-done | bytes 917536 | tf_op jit(solution)/shard_map/ppermute | solution.py:23
  42.5 1.6 constant_dynamic-update-slice_fusion.2
  44.2 1.6 constant_dynamic-update-slice_fusion.1
  45.8 9.5 %collective-permute-done.6 = bf16[1,64,2,3584]{3,2,0,1:T(2,128)(2,1)S(1)} collective-permute-done((bf16[1,64,2,3584]{3,2,0,1:T(2,128)(2,1)S(1)}, bf16[1,64,2,3584]{3,2,0,1:T(2,128)(2,1)S(1)}, u32[]{:S(2)}, u32[]{:S(2)}) %collective-permute-start.6) | collective-permute-done | bytes 917536 | tf_op jit(solution)/shard_map/ppermute | solution.py:23
  55.3 1.6 constant_dynamic-update-slice_fusion
  57.0 18.4 %all-to-all-start = ((bf16[8,64,2,3584]{3,2,0,1:T(2,128)(2,1)}), bf16[8,64,2,3584]{3,2,0,1:T(2,128)(2,1)}, u32[]{:S(2)}, u32[]{:S(2)}) async-start(bf16[8,64,2,3584]{3,2,0,1:T(2,128)(2,1)} %constant_dynamic-update-slice_fusion), calls=%async_computation | async-start | bytes 14680064 | tf_op jit(solution)/shard_map/all_to_all | solution.py:74
  75.6 322.0 %all-to-all-done = bf16[8,64,2,3584]{3,2,0,1:T(2,128)(2,1)} async-done(((bf16[8,64,2,3584]{3,2,0,1:T(2,128)(2,1)}), bf16[8,64,2,3584]{3,2,0,1:T(2,128)(2,1)}, u32[]{:S(2)}, u32[]{:S(2)}) %all-to-all-start) | async-done | bytes 7340064 | tf_op jit(solution)/shard_map/all_to_all | solution.py:74
  397.5 7.4 %copy.71 = bf16[8,64,2,3584]{3,2,1,0:T(2,128)(2,1)} copy(bf16[8,64,2,3584]{3,2,0,1:T(2,128)(2,1)} %all-to-all-done) | data formatting | bytes 14680064 | tf_op jit(solution)/shard_map/all_to_all | solution.py:74
  404.9 15.5 %reshape.62 = bf16[1024,3584]{1,0:T(8,128)(2,1)} reshape(bf16[8,64,2,3584]{3,2,1,0:T(2,128)(2,1)} %copy.71) | data formatting | bytes 14680064 | tf_op jit(solution)/shard_map/reshape | solution.py:77
  420.5 5.6 %multiply_reduce_fusion = (f32[1024]{0:T(1024)S(1)}, f32[1024,128]{0,1:T(8,128)S(1)}) fusion(bf16[1,1024,128]{1,2,0:T(8,128)(2,1)S(1)} %copy.73, bf16[1024,3584]{1,0:T(8,128)(2,1)} %reshape.62, bf16[1,128,3584]{2,1,0:T(8,128)(2,1)S(1)} %copy-done.2), kind=kOutput, calls=%fused_computation.16 | convolution fusion | flops 939916288 | bytes 9048064 | tf_op jit(solution)/shard_map/dot_general | solution.py:81
  426.1 12.6 %psum.7 = f32[8,128]{1,0:T(8,128)S(1)} all-reduce(f32[8,128]{1,0:T(8,128)S(1)} %bitcast.47), channel_id=1, replica_groups=mesh['node'=64,'local'=8] {'local'}, use_global_device_ids=true, to_apply=%region_5.6 | all-reduce | flops 1024 | bytes 8192 | tf_op jit(solution)/shard_map/psum | solution.py:97
  438.7 0.8 all_to_all.13
  439.5 9.5 %all-to-all-start.1 = ((f32[64,1,2]{2,1,0:T(1,128)}), f32[64,1,2]{2,1,0:T(1,128)}, u32[]{:S(2)}, u32[]{:S(2)}) async-start(f32[64,1,2]{2,1,0:T(1,128)} %bitcast.6), calls=%async_computation.1 | async-start | bytes 65536 | tf_op jit(solution)/shard_map/all_to_all | solution.py:99
  449.1 0.6 copy.72
  449.7 1.3 copy.82
  451.0 12.1 %all-to-all-done.1 = f32[64,1,2]{2,1,0:T(1,128)} async-done(((f32[64,1,2]{2,1,0:T(1,128)}), f32[64,1,2]{2,1,0:T(1,128)}, u32[]{:S(2)}, u32[]{:S(2)}) %all-to-all-start.1) | async-done | bytes 544 | tf_op jit(solution)/shard_map/all_to_all | solution.py:99
  463.1 0.5 broadcast.54
  463.6 1.5 reduce.7
  465.6 11.2 %all_gather.3 = bf16[8,64,2]{1,2,0:T(2,128)(2,1)S(1)} all-gather(bf16[1,64,2]{1,2,0:T(2,128)(2,1)S(1)} %copy.75), channel_id=1, replica_groups=mesh['node'=64,'local'=8] {'local'}, dimensions={0}, use_global_device_ids=true | all-gather | bytes 2304 | tf_op jit(solution)/shard_map/all_gather | solution.py:71
  476.8 0.7 copy.76
  477.6 4.6 all-to-all-start.2
  482.2 0.6 broadcast_select_fusion
  482.8 13.8 %all-to-all-done.2 = bf16[8,64,2]{0,2,1:T(2,128)(2,1)S(1)} async-done(((bf16[8,64,2]{0,2,1:T(2,128)(2,1)}), bf16[8,64,2]{0,2,1:T(2,128)(2,1)S(1)}, u32[]{:S(2)}, u32[]{:S(2)}) %all-to-all-start.2) | async-done | bytes 2080 | tf_op jit(solution)/shard_map/all_to_all | solution.py:75
  496.8 7.8 %multiply_convert_fusion = bf16[8,64,2,3584]{3,1,2,0:T(8,128)(2,1)S(1)} fusion(bf16[8,64,2,3584]{3,2,0,1:T(2,128)(2,1)} %all-to-all-done, f32[8,64,2]{1,2,0:T(2,128)S(1)} %copy.79), kind=kLoop, calls=%fused_computation | loop fusion | flops 11010048 | bytes 14684160 | tf_op jit(solution)/shard_map/convert_element_type | solution.py:86
  504.6 7.1 %copy.81 = bf16[8,64,2,3584]{3,2,1,0:T(2,128)(2,1)} copy(bf16[8,64,2,3584]{3,1,2,0:T(8,128)(2,1)S(1)} %multiply_convert_fusion) | data formatting | bytes 14680064 | tf_op jit(solution)/shard_map/convert_element_type | solution.py:86
  511.6 15.4 %convert_element_type.90 = bf16[1024,3584]{1,0:T(8,128)(2,1)} reshape(bf16[8,64,2,3584]{3,2,1,0:T(2,128)(2,1)} %copy.81) | data formatting | bytes 14680064 | tf_op jit(solution)/shard_map/convert_element_type | solution.py:86
  527.1 7.6 %fusion.5 = (bf16[1,128,3584]{1,2,0:T(8,128)(2,1)}, bf16[1,128,3584]{1,2,0:T(8,128)(2,1)}) fusion(bf16[1,128,3584]{1,2,0:T(8,128)(2,1)} %copy.82, bf16[1,128,3584]{1,2,0:T(8,128)(2,1)S(1)} %copy.72, bf16[1024,3584]{1,0:T(8,128)(2,1)} %convert_element_type.90, bf16[1,1024,128]{2,1,0:T(8,128)(2,1)S(1)} %copy-done.4), kind=kOutput, calls=%fused_computation.11 | convolution fusion | flops 946405376 | bytes 11272192 | tf_op jit(solution)/shard_map/dot_general | solution.py:87
  534.6 2.2 copy.84
  536.9 2.2 copy.85
  539.1 0.2 reshape.64
  539.3 0.8 copy.83
  (33 shorter events, 1.2 us)
Async XLA Ops:
  0.6 2.0 copy-start
  3.4 12.8 %collective-permute-start = (bf16[1,64,2,3584]{3,2,0,1:T(2,128)(2,1)S(1)}, bf16[1,64,2,3584]{3,2,0,1:T(2,128)(2,1)S(1)}, u32[]{:S(2)}, u32[]{:S(2)}) collective-permute-start(bf16[1,64,2,3584]{3,2,0,1:T(2,128)(2,1)S(1)} %bitcast.45), channel_id=1, source_target_pairs={{0,1},{1,2},{2,3},{3,4},{4,5},{5,6},{6,7},{7,0},{8,9},{9,10},{10,1... | collective-permute-start | bytes 2752520 | tf_op jit(solution)/shard_map/ppermute | solution.py:23
  3.4 12.8 %collective-permute-start.1 = (bf16[1,64,2,3584]{3,2,0,1:T(2,128)(2,1)S(1)}, bf16[1,64,2,3584]{3,2,0,1:T(2,128)(2,1)S(1)}, u32[]{:S(2)}, u32[]{:S(2)}) collective-permute-start(bf16[1,64,2,3584]{3,2,0,1:T(2,128)(2,1)S(1)} %bitcast.46), channel_id=1, source_target_pairs={{0,7},{1,0},{2,1},{3,2},{4,3},{5,4},{6,5},{7,6},{8,15},{9,8},{10,9... | collective-permute-start | bytes 2752520 | tf_op jit(solution)/shard_map/ppermute | solution.py:26
  16.2 13.5 %collective-permute-start.2 = (bf16[1,64,2,3584]{3,2,0,1:T(2,128)(2,1)S(1)}, bf16[1,64,2,3584]{3,2,0,1:T(2,128)(2,1)S(1)}, u32[]{:S(2)}, u32[]{:S(2)}) collective-permute-start(bf16[1,64,2,3584]{3,2,0,1:T(2,128)(2,1)S(1)} %collective-permute-done), channel_id=1, source_target_pairs={{0,1},{1,2},{2,3},{3,4},{4,5},{5,6},{6,7},{7,0},{8,9},{9,10},{10,1... | collective-permute-start | bytes 2752520 | tf_op jit(solution)/shard_map/ppermute | solution.py:23
  16.2 13.5 %collective-permute-start.3 = (bf16[1,64,2,3584]{3,2,0,1:T(2,128)(2,1)S(1)}, bf16[1,64,2,3584]{3,2,0,1:T(2,128)(2,1)S(1)}, u32[]{:S(2)}, u32[]{:S(2)}) collective-permute-start(bf16[1,64,2,3584]{3,2,0,1:T(2,128)(2,1)S(1)} %collective-permute-done.1), channel_id=1, source_target_pairs={{0,7},{1,0},{2,1},{3,2},{4,3},{5,4},{6,5},{7,6},{8,15},{9,8},{10,9... | collective-permute-start | bytes 2752520 | tf_op jit(solution)/shard_map/ppermute | solution.py:26
  29.7 12.8 %collective-permute-start.4 = (bf16[1,64,2,3584]{3,2,0,1:T(2,128)(2,1)S(1)}, bf16[1,64,2,3584]{3,2,0,1:T(2,128)(2,1)S(1)}, u32[]{:S(2)}, u32[]{:S(2)}) collective-permute-start(bf16[1,64,2,3584]{3,2,0,1:T(2,128)(2,1)S(1)} %collective-permute-done.2), channel_id=1, source_target_pairs={{0,1},{1,2},{2,3},{3,4},{4,5},{5,6},{6,7},{7,0},{8,9},{9,10},{10,1... | collective-permute-start | bytes 2752520 | tf_op jit(solution)/shard_map/ppermute | solution.py:23
  29.7 14.4 %collective-permute-start.5 = (bf16[1,64,2,3584]{3,2,0,1:T(2,128)(2,1)S(1)}, bf16[1,64,2,3584]{3,2,0,1:T(2,128)(2,1)S(1)}, u32[]{:S(2)}, u32[]{:S(2)}) collective-permute-start(bf16[1,64,2,3584]{3,2,0,1:T(2,128)(2,1)S(1)} %collective-permute-done.3), channel_id=1, source_target_pairs={{0,7},{1,0},{2,1},{3,2},{4,3},{5,4},{6,5},{7,6},{8,15},{9,8},{10,9... | collective-permute-start | bytes 2752520 | tf_op jit(solution)/shard_map/ppermute | solution.py:26
  42.5 12.8 %collective-permute-start.6 = (bf16[1,64,2,3584]{3,2,0,1:T(2,128)(2,1)S(1)}, bf16[1,64,2,3584]{3,2,0,1:T(2,128)(2,1)S(1)}, u32[]{:S(2)}, u32[]{:S(2)}) collective-permute-start(bf16[1,64,2,3584]{3,2,0,1:T(2,128)(2,1)S(1)} %collective-permute-done.4), channel_id=1, source_target_pairs={{0,1},{1,2},{2,3},{3,4},{4,5},{5,6},{6,7},{7,0},{8,9},{9,10},{10,1... | collective-permute-start | bytes 2752520 | tf_op jit(solution)/shard_map/ppermute | solution.py:23
  57.0 18.4 %copy-start.4 = (bf16[1,1024,128]{2,1,0:T(8,128)(2,1)S(1)}, bf16[1,1024,128]{2,1,0:T(8,128)(2,1)}, u32[]{:S(2)}) copy-start(bf16[1,1024,128]{2,1,0:T(8,128)(2,1)} %param.9) | copy-start | bytes 786436
  57.0 340.5 %all-to-all-start = ((bf16[8,64,2,3584]{3,2,0,1:T(2,128)(2,1)}), bf16[8,64,2,3584]{3,2,0,1:T(2,128)(2,1)}, u32[]{:S(2)}, u32[]{:S(2)}) async-start(bf16[8,64,2,3584]{3,2,0,1:T(2,128)(2,1)} %constant_dynamic-update-slice_fusion), calls=%async_computation | async-start | bytes 14680064 | tf_op jit(solution)/shard_map/all_to_all | solution.py:74
  404.9 15.5 %copy-start.2 = (bf16[1,128,3584]{2,1,0:T(8,128)(2,1)S(1)}, bf16[1,128,3584]{2,1,0:T(8,128)(2,1)}, u32[]{:S(2)}) copy-start(bf16[1,128,3584]{2,1,0:T(8,128)(2,1)} %param.10) | copy-start | bytes 2752516
  420.5 28.5 %copy-start.5 = (f32[128,8]{0,1:T(8,128)S(1)}, f32[128,8]{0,1:T(8,128)}, u32[]{:S(2)}) copy-start(f32[128,8]{0,1:T(8,128)} %param.8) | copy-start | bytes 12292
  420.5 29.2 %copy-start.3 = (bf16[1,128,3584]{2,1,0:T(8,128)(2,1)S(1)}, bf16[1,128,3584]{2,1,0:T(8,128)(2,1)}, u32[]{:S(2)}) copy-start(bf16[1,128,3584]{2,1,0:T(8,128)(2,1)} %param.11) | copy-start | bytes 2752516
  439.5 23.6 %all-to-all-start.1 = ((f32[64,1,2]{2,1,0:T(1,128)}), f32[64,1,2]{2,1,0:T(1,128)}, u32[]{:S(2)}, u32[]{:S(2)}) async-start(f32[64,1,2]{2,1,0:T(1,128)} %bitcast.6), calls=%async_computation.1 | async-start | bytes 65536 | tf_op jit(solution)/shard_map/all_to_all | solution.py:99
  477.6 19.0 %all-to-all-start.2 = ((bf16[8,64,2]{0,2,1:T(2,128)(2,1)}), bf16[8,64,2]{0,2,1:T(2,128)(2,1)S(1)}, u32[]{:S(2)}, u32[]{:S(2)}) async-start(bf16[8,64,2]{0,2,1:T(2,128)(2,1)} %copy.76), calls=%async_computation.2 | async-start | bytes 65536 | tf_op jit(solution)/shard_map/all_to_all | solution.py:75
  527.1 13.1 %copy-start.1 = (bf16[128,3584]{1,0:T(8,128)(2,1)S(1)}, bf16[128,3584]{1,0:T(8,128)(2,1)}, u32[]{:S(2)}) copy-start(bf16[128,3584]{1,0:T(8,128)(2,1)} %param.6) | copy-start | bytes 2752516
